TPU v7x, 512 devices: a whole 4x8x8 slice. The times are simulated.
512 devices in a mesh: req: 128 (over z, y, core), mlp: 4 (over x).
Axes of the slice: x: 4, y: 8, z: 8, core: 2. Of those that a mesh axis runs over, the one named last changes fastest.
Arguments:
- patches: bfloat16 [16384, 4, 1280], P('req', 'mlp'), may hold values from -6 to 6
- vis_gain: float32 [1280], replicated, may hold values from 0.5 to 1.5
- proj_weight: bfloat16 [4, 1280, 1280], P('mlp', 'req'), may hold values from -0.078125 to 0.078125
- image_dest: int32 [16384, 1], P('req'), may hold values from 0 to 127; in each aligned block of 128 rows (0 to 127, 128 to 255, ...) at most 2 rows name the same one
- image_pos: int32 [128], P('req'), may hold values from 0 to 255
- text_len: int32 [128], P('req'), may hold values from 64 to 255
- text: bfloat16 [128, 256, 1280], P('req'), may hold values from -6 to 6
- attn_gain: float32 [1280], replicated, may hold values from 0.5 to 1.5
- qkv_weight: bfloat16 [3, 1280, 1280], P(None, 'req', 'mlp'), may hold values from -0.15625 to 0.15625
- out_weight: bfloat16 [1280, 1280], P('mlp', 'req'), may hold values from -0.15625 to 0.15625
- cache_keys: bfloat16 [128, 1280, 1280], P('req', None, 'mlp')
- cache_values: bfloat16 [128, 1280, 1280], P('req', None, 'mlp'), may hold values from -6 to 6
- held: bfloat16 [16384, 1280], P('req'), may hold values from -6 to 6
- held_owner: int32 [128, 128, 1], P('req'), may hold values from 0 to 127; in each aligned block of 128 rows (0 to 127, 128 to 255, ..., all dimensions but the last counted through in order) at most 2 rows name the same one
- held_row: int32 [128, 128], P('req'), may hold values from 0 to 127
- recompute_pos: int32 [128, 128], P('req'), may hold values from 0 to 1279, as said below
Outputs:
- attended: bfloat16 [128, 256, 1280], P('req', None, 'mlp')
Inputs may be any that keep to these rules, and one draw needn't show every extreme that they name: `image_dest`: within each aligned block of 128 rows no request is named more than 2 times. `held_owner`: within each request's 128 rows no owner is named more than 2 times. `recompute_pos`: the positions of one request are distinct.
All inputs are finite; a program needn't handle non-finite values.
Results may differ from a plain program's by a relative error of at most 0.013.
The roundings to bfloat16 on the way count: a program that leaves them out, or rounds other values in their place, can miss the bound.
Values may be sent and summed in bfloat16 or wider, within the bound.
A program may use at most 128 MiB of HBM per device.

v0:
```python
import jax
import jax.numpy as jnp
from jax import lax
from jax.sharding import PartitionSpec as P

HEAD_DIM = 80
eps = 1e-06
big_negative = -1e30


def norm_rows(values, gain):
    floats = values.astype(jnp.float32)
    return (floats * lax.rsqrt(jnp.mean(floats * floats, -1, keepdims=True) + eps) * gain).astype(
        jnp.bfloat16
    )


def attend(queries, all_keys, all_values, length):
    seq_len = queries.shape[0]
    cache_len = all_keys.shape[0] - seq_len
    head_count = queries.shape[1] // HEAD_DIM
    query_heads = queries.reshape(seq_len, head_count, HEAD_DIM)
    key_heads = all_keys.reshape(-1, head_count, HEAD_DIM)
    value_heads = all_values.reshape(-1, head_count, HEAD_DIM)
    scores = jnp.einsum(
        "qhd,khd->hqk", query_heads, key_heads, preferred_element_type=jnp.float32
    ) * HEAD_DIM ** (-0.5)
    row_ids = jnp.arange(seq_len, dtype=jnp.int32)[:, None]
    col_ids = jnp.arange(all_keys.shape[0], dtype=jnp.int32)[None, :] - cache_len
    allowed = (col_ids < 0) | (col_ids <= row_ids) & (col_ids < length)
    scores = jnp.where(allowed[None], scores, big_negative)
    highest = jnp.max(scores, -1, keepdims=True)
    weights = jnp.exp(scores - highest)
    weights = (weights / jnp.sum(weights, -1, keepdims=True)).astype(jnp.bfloat16)
    mixed = jnp.einsum(
        "hqk,khd->qhd", weights, value_heads, preferred_element_type=jnp.float32
    ).astype(jnp.bfloat16)
    mixed = mixed.reshape(seq_len, -1)
    return jnp.where(row_ids < length, mixed, jnp.zeros_like(mixed))


def slot_ranks(targets, groups):
    onehot = (targets[:, None] == jnp.arange(groups, dtype=jnp.int32)[None, :]).astype(jnp.int32)
    before = jnp.cumsum(onehot, 0) - onehot
    return (jnp.sum(before * onehot, 1), jnp.sum(onehot, 0))


def local(
    patches,
    vis_gain,
    proj_weight,
    image_dest,
    image_pos,
    text_len,
    text,
    attn_gain,
    qkv_weight,
    out_weight,
    cache_keys,
    cache_values,
    held,
    held_owner,
    held_row,
    recompute_pos,
):
    n_req = lax.axis_size("req")
    normed_patch = norm_rows(patches[:, 0, :], vis_gain)
    partial_image = jnp.dot(
        normed_patch,
        lax.all_gather(proj_weight, "req", axis=1, tiled=True)[0],
        preferred_element_type=jnp.float32,
    )
    image_tokens = lax.psum_scatter(partial_image, "mlp", scatter_dimension=1, tiled=True).astype(
        jnp.bfloat16
    )
    img_dev = image_tokens.shape[0]
    capacity = max(2, 2 * img_dev // n_req)
    targets = image_dest[:, 0]
    image_rank, image_counts = slot_ranks(targets, n_req)
    outgoing = (
        jnp.zeros((n_req, capacity, image_tokens.shape[1]), jnp.bfloat16)
        .at[targets, image_rank]
        .set(image_tokens)
    )
    arrived, arrived_counts = (
        lax.all_to_all(outgoing, "req", split_axis=0, concat_axis=0, tiled=True),
        lax.all_to_all(
            image_counts.reshape(n_req, 1), "req", split_axis=0, concat_axis=0, tiled=True
        ),
    )
    filled = (
        (jnp.arange(capacity, dtype=jnp.int32)[None, :] < arrived_counts)
        .reshape(-1)
        .astype(jnp.int32)
    )
    image_order = jnp.cumsum(filled) - filled
    img_count = jnp.sum(filled)
    arrived_rows = arrived.reshape(n_req * capacity, arrived.shape[2])
    arrived_rows = lax.all_gather(arrived_rows, "mlp", axis=1, tiled=True)
    seq_len = text.shape[1]
    spots = jnp.arange(seq_len, dtype=jnp.int32)
    offset = jnp.minimum(image_pos[0], seq_len - img_count)
    in_image = (spots >= offset) & (spots < offset + img_count)
    chooser = ((image_order[None, :] == (spots - offset)[:, None]) & (filled[None, :] > 0)).astype(
        jnp.bfloat16
    )
    image_part = jnp.dot(chooser, arrived_rows, preferred_element_type=jnp.float32).astype(
        jnp.bfloat16
    )
    text_index = jnp.clip(jnp.where(spots < offset, spots, spots - img_count), 0, seq_len - 1)
    prompt = jnp.where(in_image[:, None], image_part, text[0][text_index])
    length = jnp.minimum(seq_len, text_len[0] + img_count)
    normed = norm_rows(prompt, attn_gain)
    weight_cols = lax.all_gather(qkv_weight, "req", axis=1, tiled=True)
    queries = jnp.dot(normed, weight_cols[0], preferred_element_type=jnp.float32).astype(
        jnp.bfloat16
    )
    new_keys = jnp.dot(normed, weight_cols[1], preferred_element_type=jnp.float32).astype(
        jnp.bfloat16
    )
    new_values = jnp.dot(normed, weight_cols[2], preferred_element_type=jnp.float32).astype(
        jnp.bfloat16
    )
    owners = held_owner[0, :, 0]
    fetch_rank, fetch_counts = slot_ranks(owners, n_req)
    recomp = owners.shape[0]
    fetch_cap = max(2, 2 * recomp // n_req)
    wanted_rows = jnp.zeros((n_req, fetch_cap), jnp.int32).at[owners, fetch_rank].set(held_row[0])
    picked = held[lax.all_to_all(wanted_rows, "req", split_axis=0, concat_axis=0, tiled=True)]
    fetched = lax.all_to_all(picked, "req", split_axis=0, concat_axis=0, tiled=True)
    gotten = fetched[owners, fetch_rank]
    held_norm = norm_rows(gotten, attn_gain)
    fresh_keys = jnp.dot(held_norm, weight_cols[1], preferred_element_type=jnp.float32).astype(
        jnp.bfloat16
    )
    fresh_values = jnp.dot(held_norm, weight_cols[2], preferred_element_type=jnp.float32).astype(
        jnp.bfloat16
    )
    keys_now = cache_keys[0].at[recompute_pos[0]].set(fresh_keys)
    values_now = cache_values[0].at[recompute_pos[0]].set(fresh_values)
    mixed = attend(
        queries,
        jnp.concatenate([keys_now, new_keys], 0),
        jnp.concatenate([values_now, new_values], 0),
        length,
    )
    terms = jnp.dot(
        mixed,
        lax.all_gather(out_weight, "req", axis=1, tiled=True),
        preferred_element_type=jnp.float32,
    )
    result = lax.psum_scatter(terms, "mlp", scatter_dimension=1, tiled=True).astype(jnp.bfloat16)
    return result[None]


def solution(mesh):
    in_specs = (
        P("req", "mlp", None),
        P(),
        P("mlp", "req", None),
        P("req", None),
        P("req"),
        P("req"),
        P("req", None, None),
        P(),
        P(None, "req", "mlp"),
        P("mlp", "req"),
        P("req", None, "mlp"),
        P("req", None, "mlp"),
        P("req", None),
        P("req", None, None),
        P("req", None),
        P("req", None),
    )
    out_specs = P("req", None, "mlp")
    return jax.shard_map(local, mesh=mesh, in_specs=in_specs, out_specs=out_specs, check_vma=False)
```

profile of v0, /device:TPU:8, one launch (start us, length us, event | category | flops | bytes accessed | tf_op | source)
XLA Modules:
  0.0 346.3 jit_solution(4919640971527965085)
XLA Ops:
  11.4 17.4 %all-to-all-start = ((s32[128,1,1]{2,1,0:T(1,128)}), s32[128,1,1]{2,1,0:T(1,128)S(1)}, u32[]{:S(2)}, u32[]{:S(2)}) async-start(s32[128,1,1]{2,1,0:T(1,128)} %copy.44), calls=%async_computation | async-start | bytes 131072 | tf_op jit(solution)/shard_map/all_to_all | solution.py:87
  31.7 52.4 %all-gather = bf16[128,10,320]{2,1,0:T(8,128)(2,1)S(1)} all-gather(bf16[1,10,320]{2,1,0:T(8,128)(2,1)} %bitcast.98), channel_id=1, replica_groups=mesh['req'=128,'mlp'=4] {'req'}, dimensions={0}, use_global_device_ids=true | all-gather | bytes 825600 | tf_op jit(solution)/shard_map/all_gather | solution.py:149
  85.5 6.4 %scatter_fusion = s32[128,2]{0,1:T(2,128)S(1)} fusion(s32[128,2]{0,1:T(2,128)S(1)} %broadcast.276, s32[128]{0:T(128)S(1)} %get-tuple-element.7, s32[128]{0:T(128)S(1)} %bitcast.105), kind=kCustom, calls=%fused_computation.3 | custom fusion | bytes 2560 | tf_op jit(solution)/shard_map/scatter | solution.py:128
  94.5 2.3 copy.45
  98.2 10.5 %all-to-all-start.1 = ((s32[128,1,2]{2,1,0:T(1,128)}), s32[128,1,2]{2,1,0:T(1,128)S(1)}, u32[]{:S(2)}, u32[]{:S(2)}) async-start(s32[128,1,2]{2,1,0:T(1,128)} %copy.46), calls=%async_computation.1 | async-start | bytes 131072 | tf_op jit(solution)/shard_map/all_to_all | solution.py:129
  108.7 2.4 reduce.2
  113.6 5.9 %all-to-all-done.1 = s32[128,1,2]{2,1,0:T(1,128)S(1)} async-done(((s32[128,1,2]{2,1,0:T(1,128)}), s32[128,1,2]{2,1,0:T(1,128)S(1)}, u32[]{:S(2)}, u32[]{:S(2)}) %all-to-all-start.1) | async-done | bytes 1056 | tf_op jit(solution)/shard_map/all_to_all | solution.py:129
  122.0 7.8 %all-to-all-start.2 = ((bf16[128,2,1280]{2,1,0:T(2,128)(2,1)}), bf16[128,2,1280]{2,1,0:T(2,128)(2,1)S(1)}, u32[]{:S(2)}, u32[]{:S(2)}) async-start(bf16[128,2,1280]{2,1,0:T(2,128)(2,1)} %reshape.343), calls=%async_computation.2 | async-start | bytes 1310720 | tf_op jit(solution)/shard_map/all_to_all | solution.py:130
  136.7 16.5 %all-to-all-done.2 = bf16[128,2,1280]{2,1,0:T(2,128)(2,1)S(1)} async-done(((bf16[128,2,1280]{2,1,0:T(2,128)(2,1)}), bf16[128,2,1280]{2,1,0:T(2,128)(2,1)S(1)}, u32[]{:S(2)}, u32[]{:S(2)}) %all-to-all-start.2) | async-done | bytes 655392 | tf_op jit(solution)/shard_map/all_to_all | solution.py:130
  155.4 5.1 %fusion.2 = f32[128,1280]{0,1:T(8,128)} fusion(bf16[1,1280,1280]{2,0,1:T(2,128)(2,1)} %all-gather.6.cloned.1.call-done, bf16[128,1,1280]{2,0,1:T(8,128)(2,1)S(1)} %copy-done.15, f32[1280]{0:T(1024)S(1)} %copy-done.26, f32[128]{0:T(128)S(1)} %add_rsqrt_fusion.1), kind=kOutput, calls=%fused_computation.12 | convolution fusion | flops 420085760 | bytes 4265472 | tf_op jit(solution)/shard_map/dot_general | solution.py:68
  160.5 33.4 %all-gather.4.cloned.1.call-done = bf16[3,1280,320]{2,0,1:T(4,128)(2,1)} async-done(((bf16[3,10,320]{2,0,1:T(4,128)(2,1)}), bf16[3,1280,320]{2,0,1:T(4,128)(2,1)}) %all-gather.4.cloned.1.call-update) | async-done | bytes 2457616 | tf_op jit(solution)/shard_map/all_gather | solution.py:114
  194.0 10.7 %fusion.59 = (bf16[1,1280,320]{2,0,1:T(2,128)(2,1)}, bf16[1,1280,320]{2,0,1:T(2,128)(2,1)}, bf16[1,1280,320]{2,0,1:T(2,128)(2,1)S(1)}) fusion(bf16[3,1280,320]{2,0,1:T(4,128)(2,1)} %all-gather.4.cloned.1.call-done), kind=kLoop, calls=%fused_computation.111 | loop fusion | bytes 4915200 | tf_op jit(solution)/shard_map/slice | solution.py:133
  204.7 3.9 %copy.63 = bf16[1,1280,320]{1,2,0:T(8,128)(2,1)S(1)} copy(bf16[1,1280,320]{2,0,1:T(2,128)(2,1)} %get-tuple-element.9) | data formatting | bytes 1638400
  208.6 12.9 %reduce-scatter.3.cloned.1.call-done = f32[128,320]{0,1:T(8,128)} async-done(((f32[128,1280]{0,1:T(8,128)}), f32[128,320]{0,1:T(8,128)}) %reduce-scatter.3.cloned.1.call-update) | async-done | bytes 163856 | tf_op jit(solution)/shard_map/reduce_scatter | solution.py:73
  224.8 15.1 %scatter_fusion.2 = bf16[128,2,320]{2,1,0:T(2,128)(2,1)} fusion(bf16[128,2,320]{2,1,0:T(2,128)(2,1)} %broadcast_in_dim.29, s32[128]{0:T(128)S(1)} %fusion.50, bf16[128,320]{1,0:T(8,128)(2,1)S(1)} %copy.50), kind=kCustom, calls=%fused_computation.5 | custom fusion | bytes 246784 | tf_op jit(solution)/shard_map/scatter | solution.py:83
  239.9 14.7 %all-to-all-start.3 = ((bf16[128,2,320]{2,1,0:T(2,128)(2,1)}), bf16[128,2,320]{2,1,0:T(2,128)(2,1)}, u32[]{:S(2)}, u32[]{:S(2)}) async-start(bf16[128,2,320]{2,1,0:T(2,128)(2,1)} %scatter_fusion.2), calls=%async_computation.4 | async-start | bytes 393216 | tf_op jit(solution)/shard_map/all_to_all | solution.py:86
  257.7 4.9 %copy.62 = bf16[1,1280,320]{1,2,0:T(8,128)(2,1)} copy(bf16[1,1280,320]{2,0,1:T(2,128)(2,1)} %get-tuple-element.10) | data formatting | bytes 1638400
  262.6 2.8 copy.61
  267.3 3.5 %scatter_fusion.3 = bf16[1280,320]{1,0:T(8,128)(2,1)} fusion(bf16[1280,320]{1,0:T(8,128)(2,1)} %bitcast.91, s32[128]{0:T(128)} %fusion.48, bf16[128,320]{1,0:T(8,128)(2,1)S(1)} %copy.57), kind=kCustom, calls=%fused_computation.6 | custom fusion | bytes 246272 | tf_op jit(solution)/shard_map/scatter | solution.py:139
  273.7 13.8 %all_gather.14 = bf16[256,1280]{0,1:T(8,128)(2,1)S(1)} all-gather(bf16[256,320]{0,1:T(8,128)(2,1)S(1)} %copy.51), channel_id=1, replica_groups=mesh['req'=128,'mlp'=4] {'mlp'}, dimensions={1}, use_global_device_ids=true | all-gather | bytes 819200 | tf_op jit(solution)/shard_map/all_gather | solution.py:99
  293.0 2.4 copy.59
  299.3 3.7 %fusion.60 = f32[4,256]{1,0:T(4,128)S(1)} fusion(pred[256,1536]{1,0:T(8,128)(4,1)S(1)} %copy-done.14, bf16[256,4,80]{0,2,1:T(8,128)(2,1)} %bitcast.96, bf16[1536,4,80]{0,2,1:T(8,128)(2,1)} %bitcast.92), kind=kOutput, calls=%fused_computation.112 | convolution fusion | flops 257951232 | bytes 1544192 | tf_op jit(solution)/shard_map/sub | solution.py:33
  303.1 3.9 %fusion.13 = bf16[4,80,256]{2,1,0:T(8,128)(2,1)S(1)} fusion(bf16[1536,4,80]{0,2,1:T(8,128)(2,1)} %bitcast.94, f32[4,256]{1,0:T(4,128)S(1)} %fusion.60, pred[256,1536]{1,0:T(8,128)(4,1)S(1)} %copy-done.14, bf16[256,4,80]{0,2,1:T(8,128)(2,1)S(1)} %bitcast.97, bf16[1536,4,80]{0,2,1:T(8,128)(2,1)S(1)} %bitcast.93), kind=kOutput, calls=%fused_computation.29 | convolution fusion | flops 511265280 | bytes 2691072 | tf_op jit(solution)/shard_map/hqk,khd->qhd/dot_general | solution.py:35
  308.7 29.4 %reduce-scatter.5.cloned.1.call-done = f32[256,320]{0,1:T(8,128)} async-done(((f32[256,1280]{0,1:T(8,128)}), f32[256,320]{0,1:T(8,128)}) %reduce-scatter.5.cloned.1.call-update) | async-done | bytes 327696 | tf_op jit(solution)/shard_map/reduce_scatter | solution.py:152
  (138 shorter events, 47.6 us)
Async XLA Ops:
  6.5 125.2 %copy-start = (bf16[1,256,1280]{2,1,0:T(8,128)(2,1)S(1)}, bf16[1,256,1280]{2,1,0:T(8,128)(2,1)}, u32[]{:S(2)}) copy-start(bf16[1,256,1280]{2,1,0:T(8,128)(2,1)} %param.22) | copy-start | bytes 1966084
  6.5 78.1 %copy-start.20 = (s32[128,1]{0,1:T(1,128)S(1)}, s32[128,1]{0,1:T(1,128)}, u32[]{:S(2)}) copy-start(s32[128,1]{0,1:T(1,128)} %param.19) | copy-start | bytes 1540
  6.5 78.1 %copy-start.18 = (s32[1,128,1]{1,2,0:T(1,128)S(1)}, s32[1,128,1]{1,2,0:T(1,128)}, u32[]{:S(2)}) copy-start(s32[1,128,1]{1,2,0:T(1,128)} %param.29) | copy-start | bytes 1540
  6.5 77.6 %copy-start.27 = (s32[1,128]{1,0:T(1,128)S(1)}, s32[1,128]{1,0:T(1,128)}, u32[]{:S(2)}) copy-start(s32[1,128]{1,0:T(1,128)} %param.31) | copy-start | bytes 1540
  6.5 78.9 %copy-start.24 = (s32[1,128]{1,0:T(1,128)S(1)}, s32[1,128]{1,0:T(1,128)}, u32[]{:S(2)}) copy-start(s32[1,128]{1,0:T(1,128)} %param.30) | copy-start | bytes 1540
  6.5 86.0 %copy-start.12 = (bf16[1,1280,320]{1,2,0:T(8,128)(2,1)S(1)}, bf16[1,1280,320]{1,2,0:T(8,128)(2,1)}, u32[]{:S(2)}) copy-start(bf16[1,1280,320]{1,2,0:T(8,128)(2,1)} %param.26) | copy-start | bytes 2457604
  6.6 148.8 %all-gather.6.cloned.1.call-start = ((), (), s32[]{:S(2)}) async-start(), calls=%async_computation.7 | async-start | bytes 6604800 | tf_op jit(solution)/shard_map/all_gather | solution.py:70
  8.2 185.8 %all-gather.4.cloned.1.call-start = ((), (), s32[]{:S(2)}) async-start(), calls=%async_computation.6 | async-start | bytes 3962880 | tf_op jit(solution)/shard_map/all_gather | solution.py:114
  11.4 86.8 %all-to-all-start = ((s32[128,1,1]{2,1,0:T(1,128)}), s32[128,1,1]{2,1,0:T(1,128)S(1)}, u32[]{:S(2)}, u32[]{:S(2)}) async-start(s32[128,1,1]{2,1,0:T(1,128)} %copy.44), calls=%async_computation | async-start | bytes 131072 | tf_op jit(solution)/shard_map/all_to_all | solution.py:87
  94.5 25.1 %copy-start.1 = (bf16[128,1280]{1,0:T(8,128)(2,1)S(1)}, bf16[128,1280]{1,0:T(8,128)(2,1)}, u32[]{:S(2)}) copy-start(bf16[128,1280]{1,0:T(8,128)(2,1)} %param.28) | copy-start | bytes 983044
  98.2 21.2 %all-to-all-start.1 = ((s32[128,1,2]{2,1,0:T(1,128)}), s32[128,1,2]{2,1,0:T(1,128)S(1)}, u32[]{:S(2)}, u32[]{:S(2)}) async-start(s32[128,1,2]{2,1,0:T(1,128)} %copy.46), calls=%async_computation.1 | async-start | bytes 131072 | tf_op jit(solution)/shard_map/all_to_all | solution.py:129
  122.0 31.2 %all-to-all-start.2 = ((bf16[128,2,1280]{2,1,0:T(2,128)(2,1)}), bf16[128,2,1280]{2,1,0:T(2,128)(2,1)S(1)}, u32[]{:S(2)}, u32[]{:S(2)}) async-start(bf16[128,2,1280]{2,1,0:T(2,128)(2,1)} %reshape.343), calls=%async_computation.2 | async-start | bytes 1310720 | tf_op jit(solution)/shard_map/all_to_all | solution.py:130
  129.8 91.6 %reduce-scatter.3.cloned.1.call-start = ((), (), s32[]{:S(2)}) async-start(), calls=%async_computation.8 | async-start | bytes 819200 | tf_op jit(solution)/shard_map/reduce_scatter | solution.py:73
  133.9 21.5 %copy-start.15 = (bf16[128,1,1280]{2,0,1:T(8,128)(2,1)S(1)}, bf16[128,1,1280]{2,0,1:T(8,128)(2,1)}, u32[]{:S(2)}) copy-start(bf16[128,1,1280]{2,0,1:T(8,128)(2,1)} %param.16) | copy-start | bytes 983044
  133.9 21.5 %copy-start.26 = (f32[1280]{0:T(1024)S(1)}, f32[1280]{0:T(1024)}, u32[]{:S(2)}) copy-start(f32[1280]{0:T(1024)} %param.17) | copy-start | bytes 15364
  204.7 50.0 %copy-start.17 = (f32[1280]{0:T(1024)S(1)}, f32[1280]{0:T(1024)}, u32[]{:S(2)}) copy-start(f32[1280]{0:T(1024)} %param.23) | copy-start | bytes 15364
  208.6 54.0 %copy-start.5 = (bf16[1,1280,320]{1,2,0:T(8,128)(2,1)}, bf16[1,1280,320]{1,2,0:T(8,128)(2,1)S(1)}, u32[]{:S(2)}) copy-start(bf16[1,1280,320]{1,2,0:T(8,128)(2,1)S(1)} %copy.63) | copy-start | bytes 2457604
  239.9 32.6 %all-to-all-start.3 = ((bf16[128,2,320]{2,1,0:T(2,128)(2,1)}), bf16[128,2,320]{2,1,0:T(2,128)(2,1)}, u32[]{:S(2)}, u32[]{:S(2)}) async-start(bf16[128,2,320]{2,1,0:T(2,128)(2,1)} %scatter_fusion.2), calls=%async_computation.4 | async-start | bytes 393216 | tf_op jit(solution)/shard_map/all_to_all | solution.py:86
  254.6 83.5 %reduce-scatter.5.cloned.1.call-start = ((), (), s32[]{:S(2)}) async-start(), calls=%async_computation.9 | async-start | bytes 1638400 | tf_op jit(solution)/shard_map/reduce_scatter | solution.py:152
  265.4 7.1 %copy-start.7 = (bf16[1,1280,320]{1,2,0:T(8,128)(2,1)}, bf16[1,1280,320]{1,2,0:T(8,128)(2,1)S(1)}, u32[]{:S(2)}) copy-start(bf16[1,1280,320]{1,2,0:T(8,128)(2,1)S(1)} %copy.61) | copy-start | bytes 2457604
  267.3 20.2 %copy-start.9 = (bf16[256,1280]{1,0:T(8,128)(2,1)S(1)}, bf16[256,1280]{1,0:T(8,128)(2,1)}, u32[]{:S(2)}) copy-start(bf16[256,1280]{1,0:T(8,128)(2,1)} %gather_fusion.2) | copy-start | bytes 1966084
  270.8 16.7 %copy-start.19 = (s32[256]{0:T(256)S(1)}, s32[256]{0:T(256)}, u32[]{:S(2)}) copy-start(s32[256]{0:T(256)} %get-tuple-element.17) | copy-start | bytes 3076
  270.8 16.7 %copy-start.22 = (pred[256]{0:T(512)(128)(4,1)S(1)}, pred[256]{0:T(512)(128)(4,1)}, u32[]{:S(2)}) copy-start(pred[256]{0:T(512)(128)(4,1)} %get-tuple-element.14) | copy-start | bytes 772
  270.8 16.7 %copy-start.23 = (pred[256]{0:T(512)(128)(4,1)S(1)}, pred[256]{0:T(512)(128)(4,1)}, u32[]{:S(2)}) copy-start(pred[256]{0:T(512)(128)(4,1)} %get-tuple-element.15) | copy-start | bytes 772
  (12 other events, 45.2 us)
Sparse Core Ops, SparseCore 0:
  10.6 91.5 all-gather.5
  105.4 88.5 all-gather.3
  196.8 24.6 reduce-scatter.2
  308.8 29.2 reduce-scatter.4
where the time goes:
time: 348 us; the launch traced here: 346 us
  waiting for transfers between devices  98.9 us (28%)
  local copies, waits for them, and re-layouts  73.4 us (21%)
  blocking collectives  66.2 us (19%)
  starting transfers between devices  50.5 us (15%)
  matrix products  23 us (7%)
  other arithmetic  17.4 us (5%)
  between operations  16.9 us (5%)
    all_gather x1, blocking collectives, local(): lax.all_gather(out_weight, 'req', axis=1, tiled=True)  52.4 us
    all_gather x1, waiting for transfers between devices, local(): weight_cols = lax.all_gather(qkv_weight, 'req', axis=1, tiled=True)  33.4 us
    reduce_scatter x1, waiting for transfers between devices, local(): lax.psum_scatter(terms, 'mlp', scatter_dimension=1, tiled=True)  29.4 us
    unnamed x63, local copies, waits for them, and re-layouts  18.6 us
    all_to_all x1, starting transfers between devices, local(): lax.all_to_all(image_counts.reshape(n_req, 1), 'req', split_axis=0, conca...  17.4 us
    all_to_all x1, waiting for transfers between devices, local(): lax.all_to_all(picked, 'req', split_axis=0, concat_axis=0, tiled=True)  16.5 us
    scatter x1, local copies, waits for them, and re-layouts, local(): outgoing = jnp.zeros((n_req, capacity, image_tokens.shape[1]), jnp.bfloat...  15.1 us
    all_to_all x1, starting transfers between devices, local(): lax.all_to_all(outgoing, 'req', split_axis=0, concat_axis=0, tiled=True)  14.7 us
  transfers between devices with their start and end apart: 8, of which 5 were waited for; matrix products, arithmetic and copies ran while one was open for 20% of the time, Pallas kernels for 0%

commit v1 on v0

--- a/solution.py
+++ b/solution.py
@@ -6,6 +6,11 @@
 HEAD_DIM = 80
 eps = 1e-06
 big_negative = -1e30
+
+
+def exchange_gather(block, mesh_axis, dim):
+    sent = jnp.stack([block] * lax.axis_size(mesh_axis))
+    return jnp.concatenate(lax.all_to_all(sent, mesh_axis, 0, 0), axis=dim)
 
 
 def norm_rows(values, gain):
@@ -145,9 +150,7 @@
         length,
     )
     terms = jnp.dot(
-        mixed,
-        lax.all_gather(out_weight, "req", axis=1, tiled=True),
-        preferred_element_type=jnp.float32,
+        mixed, exchange_gather(out_weight, "req", 1), preferred_element_type=jnp.float32
     )
     result = lax.psum_scatter(terms, "mlp", scatter_dimension=1, tiled=True).astype(jnp.bfloat16)
     return result[None]

time: 348 us -> 366 us (1.052)
  waiting for transfers between devices: 98.9 us -> 157 us
  blocking collectives: 66.2 us -> 13.8 us
  starting transfers between devices: 50.5 us -> 57.1 us
  local copies, waits for them, and re-layouts: 73.4 us -> 78.4 us
    all_gather x1 -> x0, blocking collectives: 52.4 us -> none  [local(): lax.all_gather(out_weight, 'req', axis=1, tiled=True)]
    all_to_all x0 -> x1, waiting for transfers between devices: none -> 33.7 us  [exchange_gather(): return jnp.concatenate(lax.all_to_all(sent, mesh_axis, 0, 0), axis=dim)]
    all_gather x1, waiting for transfers between devices: 33.4 us -> 46.9 us  [local(): weight_cols = lax.all_gather(qkv_weight, 'req', axis=1, tiled=True)]
    all_to_all x1, waiting for transfers between devices: 0.01 us -> 8.16 us  [local(): lax.all_to_all(image_counts.reshape(n_req, 1), 'req', split_axis=0, conca...]
    all_to_all x0 -> x1, starting transfers between devices: none -> 7.74 us  [exchange_gather(): return jnp.concatenate(lax.all_to_all(sent, mesh_axis, 0, 0), axis=dim)]
    all_to_all x1, starting transfers between devices: 10.5 us -> 17.4 us  [local(): lax.all_to_all(wanted_rows, 'req', split_axis=0, concat_axis=0, tiled=True)]
    all_to_all x1, starting transfers between devices: 17.4 us -> 10.8 us  [local(): lax.all_to_all(image_counts.reshape(n_req, 1), 'req', split_axis=0, conca...]
    all_to_all x1, waiting for transfers between devices: 16.5 us -> 21.9 us  [local(): lax.all_to_all(picked, 'req', split_axis=0, concat_axis=0, tiled=True)]
  transfers between devices with their start and end apart: 8 -> 9, of which waited for: 5 -> 7; matrix products, arithmetic and copies ran while one was open for 20% -> 21% of each run, Pallas kernels for 0% -> 0%
where the time goes in v1:
time: 366 us; the launch traced here: 365 us
  waiting for transfers between devices  157 us (43%)
  local copies, waits for them, and re-layouts  78.4 us (21%)
  starting transfers between devices  57.1 us (16%)
  matrix products  23 us (6%)
  other arithmetic  18.9 us (5%)
  between operations  16.9 us (5%)
  blocking collectives  13.8 us (4%)
    all_gather x1, waiting for transfers between devices, local(): weight_cols = lax.all_gather(qkv_weight, 'req', axis=1, tiled=True)  46.9 us
    all_to_all x1, waiting for transfers between devices, exchange_gather(): return jnp.concatenate(lax.all_to_all(sent, mesh_axis, 0, 0), axis=dim)  33.7 us
    reduce_scatter x1, waiting for transfers between devices, local(): lax.psum_scatter(terms, 'mlp', scatter_dimension=1, tiled=True)  29.4 us
    all_to_all x1, waiting for transfers between devices, local(): lax.all_to_all(picked, 'req', split_axis=0, concat_axis=0, tiled=True)  21.9 us
    all_to_all x1, starting transfers between devices, local(): lax.all_to_all(wanted_rows, 'req', split_axis=0, concat_axis=0, tiled=True)  17.4 us
    unnamed x68, local copies, waits for them, and re-layouts  16.3 us
    scatter x1, local copies, waits for them, and re-layouts, local(): outgoing = jnp.zeros((n_req, capacity, image_tokens.shape[1]), jnp.bfloat...  15.1 us
    all_to_all x1, starting transfers between devices, local(): lax.all_to_all(outgoing, 'req', split_axis=0, concat_axis=0, tiled=True)  14.4 us
  transfers between devices with their start and end apart: 9, of which 7 were waited for; matrix products, arithmetic and copies ran while one was open for 21% of the time, Pallas kernels for 0%

profile of v1, /device:TPU:8, one launch (start us, length us, event | category | flops | bytes accessed | tf_op | source)
XLA Modules:
  0.0 364.7 jit_solution(17063799169374356126)
XLA Ops:
  11.3 11.0 %scatter_fusion = s32[128,2]{0,1:T(2,128)S(1)} fusion(s32[128,2]{0,1:T(2,128)S(1)} %broadcast.286, s32[128]{0:T(128)S(1)} %get-tuple-element.7, s32[128]{0:T(128)} %bitcast.105), kind=kCustom, calls=%fused_computation.3 | custom fusion | bytes 2560 | tf_op jit(solution)/shard_map/scatter | solution.py:133
  23.0 17.4 %all-to-all-start.1 = ((s32[128,1,2]{2,1,0:T(1,128)}), s32[128,1,2]{2,1,0:T(1,128)S(1)}, u32[]{:S(2)}, u32[]{:S(2)}) async-start(s32[128,1,2]{2,1,0:T(1,128)} %copy.47), calls=%async_computation.1 | async-start | bytes 131072 | tf_op jit(solution)/shard_map/all_to_all | solution.py:134
  48.2 2.9 all-to-all-done.1
  51.1 10.8 %all-to-all-start = ((s32[128,1,1]{2,1,0:T(1,128)}), s32[128,1,1]{2,1,0:T(1,128)S(1)}, u32[]{:S(2)}, u32[]{:S(2)}) async-start(s32[128,1,1]{2,1,0:T(1,128)} %copy.45), calls=%async_computation | async-start | bytes 131072 | tf_op jit(solution)/shard_map/all_to_all | solution.py:92
  64.5 8.2 %all-to-all-done = s32[128,1,1]{2,1,0:T(1,128)S(1)} async-done(((s32[128,1,1]{2,1,0:T(1,128)}), s32[128,1,1]{2,1,0:T(1,128)S(1)}, u32[]{:S(2)}, u32[]{:S(2)}) %all-to-all-start) | async-done | bytes 544 | tf_op jit(solution)/shard_map/all_to_all | solution.py:92
  72.7 6.4 %all-to-all-start.2 = ((bf16[128,2,1280]{2,1,0:T(2,128)(2,1)}), bf16[128,2,1280]{2,1,0:T(2,128)(2,1)S(1)}, u32[]{:S(2)}, u32[]{:S(2)}) async-start(bf16[128,2,1280]{2,1,0:T(2,128)(2,1)} %reshape.356), calls=%async_computation.2 | async-start | bytes 1310720 | tf_op jit(solution)/shard_map/all_to_all | solution.py:135
  85.1 21.9 %all-to-all-done.2 = bf16[128,2,1280]{2,1,0:T(2,128)(2,1)S(1)} async-done(((bf16[128,2,1280]{2,1,0:T(2,128)(2,1)}), bf16[128,2,1280]{2,1,0:T(2,128)(2,1)S(1)}, u32[]{:S(2)}, u32[]{:S(2)}) %all-to-all-start.2) | async-done | bytes 655392 | tf_op jit(solution)/shard_map/all_to_all | solution.py:135
  108.3 7.7 %all-to-all-start.4 = ((bf16[128,320,10]{1,2,0:T(8,128)(2,1)}), bf16[128,320,10]{1,2,0:T(8,128)(2,1)S(1)}, u32[]{:S(2)}, u32[]{:S(2)}) async-start(bf16[128,320,10]{1,2,0:T(8,128)(2,1)} %stack.2), calls=%async_computation.5 | async-start | bytes 3145728 | tf_op jit(solution)/shard_map/all_to_all | solution.py:13
  125.3 33.7 %all-to-all-done.4 = bf16[128,320,10]{1,2,0:T(8,128)(2,1)S(1)} async-done(((bf16[128,320,10]{1,2,0:T(8,128)(2,1)}), bf16[128,320,10]{1,2,0:T(8,128)(2,1)S(1)}, u32[]{:S(2)}, u32[]{:S(2)}) %all-to-all-start.4) | async-done | bytes 819232 | tf_op jit(solution)/shard_map/all_to_all | solution.py:13
  160.4 5.1 %fusion.2 = f32[128,1280]{0,1:T(8,128)} fusion(bf16[1,1280,1280]{2,0,1:T(2,128)(2,1)} %all-gather.5.cloned.1.call-done, bf16[128,1,1280]{2,0,1:T(8,128)(2,1)S(1)} %copy-done.16, f32[1280]{0:T(1024)S(1)} %copy-done.26, f32[128]{0:T(128)S(1)} %copy-done.29), kind=kOutput, calls=%fused_computation.12 | convolution fusion | flops 420085760 | bytes 4265472 | tf_op jit(solution)/shard_map/dot_general | solution.py:73
  165.6 46.9 %all-gather.3.cloned.1.call-done = bf16[3,1280,320]{2,0,1:T(4,128)(2,1)} async-done(((bf16[3,10,320]{2,0,1:T(4,128)(2,1)}), bf16[3,1280,320]{2,0,1:T(4,128)(2,1)}) %all-gather.3.cloned.1.call-update) | async-done | bytes 2457616 | tf_op jit(solution)/shard_map/all_gather | solution.py:119
  212.5 10.7 %fusion.60 = (bf16[1,1280,320]{2,0,1:T(2,128)(2,1)}, bf16[1,1280,320]{2,0,1:T(2,128)(2,1)}, bf16[1,1280,320]{2,0,1:T(2,128)(2,1)S(1)}) fusion(bf16[3,1280,320]{2,0,1:T(4,128)(2,1)} %all-gather.3.cloned.1.call-done), kind=kLoop, calls=%fused_computation.111 | loop fusion | bytes 4915200 | tf_op jit(solution)/shard_map/slice | solution.py:138
  223.2 3.9 %copy.64 = bf16[1,1280,320]{1,2,0:T(8,128)(2,1)S(1)} copy(bf16[1,1280,320]{2,0,1:T(2,128)(2,1)} %get-tuple-element.9) | data formatting | bytes 1638400
  227.1 12.9 %reduce-scatter.3.cloned.1.call-done = f32[128,320]{0,1:T(8,128)} async-done(((f32[128,1280]{0,1:T(8,128)}), f32[128,320]{0,1:T(8,128)}) %reduce-scatter.3.cloned.1.call-update) | async-done | bytes 163856 | tf_op jit(solution)/shard_map/reduce_scatter | solution.py:78
  243.3 15.1 %scatter_fusion.2 = bf16[128,2,320]{2,1,0:T(2,128)(2,1)} fusion(bf16[128,2,320]{2,1,0:T(2,128)(2,1)} %broadcast_in_dim.29, s32[128]{0:T(128)S(1)} %fusion.51, bf16[128,320]{1,0:T(8,128)(2,1)S(1)} %copy.51), kind=kCustom, calls=%fused_computation.5 | custom fusion | bytes 246784 | tf_op jit(solution)/shard_map/scatter | solution.py:88
  258.4 14.4 %all-to-all-start.3 = ((bf16[128,2,320]{2,1,0:T(2,128)(2,1)}), bf16[128,2,320]{2,1,0:T(2,128)(2,1)}, u32[]{:S(2)}, u32[]{:S(2)}) async-start(bf16[128,2,320]{2,1,0:T(2,128)(2,1)} %scatter_fusion.2), calls=%async_computation.4 | async-start | bytes 393216 | tf_op jit(solution)/shard_map/all_to_all | solution.py:91
  276.2 4.9 %copy.63 = bf16[1,1280,320]{1,2,0:T(8,128)(2,1)} copy(bf16[1,1280,320]{2,0,1:T(2,128)(2,1)} %get-tuple-element.10) | data formatting | bytes 1638400
  281.0 2.8 copy.62
  285.7 3.5 scatter_fusion.3
  292.2 13.8 %all_gather.11 = bf16[256,1280]{0,1:T(8,128)(2,1)S(1)} all-gather(bf16[256,320]{0,1:T(8,128)(2,1)S(1)} %copy.52), channel_id=1, replica_groups=mesh['req'=128,'mlp'=4] {'mlp'}, dimensions={1}, use_global_device_ids=true | all-gather | bytes 819200 | tf_op jit(solution)/shard_map/all_gather | solution.py:104
  311.5 2.4 copy.60
  317.8 3.7 %fusion.61 = f32[4,256]{1,0:T(4,128)S(1)} fusion(pred[256,1536]{1,0:T(8,128)(4,1)S(1)} %copy-done.15, bf16[256,4,80]{0,2,1:T(8,128)(2,1)} %bitcast.97, bf16[1536,4,80]{0,2,1:T(8,128)(2,1)} %bitcast.92), kind=kOutput, calls=%fused_computation.112 | convolution fusion | flops 257951232 | bytes 1544192 | tf_op jit(solution)/shard_map/sub | solution.py:38
  321.6 3.9 %fusion.14 = bf16[4,80,256]{2,1,0:T(8,128)(2,1)S(1)} fusion(bf16[1536,4,80]{0,2,1:T(8,128)(2,1)} %bitcast.94, f32[4,256]{1,0:T(4,128)S(1)} %fusion.61, pred[256]{0:T(512)(128)(4,1)S(1)} %copy-done.28, pred[256,1536]{1,0:T(8,128)(4,1)S(1)} %copy-done.15, bf16[256,4,80]{0,2,1:T(8,128)(2,1)S(1)} %bitcast.98, bf16[1536,4,80]{0,2,1:T(8,128)(2,1)S(1)} %bitcast.93), kind=kOutput, calls=%fused_computation.35 | convolution fusion | flops 511347200 | bytes 2691328 | tf_op jit(solution)/shard_map/hqk,khd->qhd/dot_general | solution.py:40
  327.1 29.4 %reduce-scatter.5.cloned.1.call-done = f32[256,320]{0,1:T(8,128)} async-done(((f32[256,1280]{0,1:T(8,128)}), f32[256,320]{0,1:T(8,128)}) %reduce-scatter.5.cloned.1.call-update) | async-done | bytes 327696 | tf_op jit(solution)/shard_map/reduce_scatter | solution.py:155
  (145 shorter events, 54.5 us)
Async XLA Ops:
  6.5 111.4 %copy-start = (bf16[1,256,1280]{2,1,0:T(8,128)(2,1)S(1)}, bf16[1,256,1280]{2,1,0:T(8,128)(2,1)}, u32[]{:S(2)}) copy-start(bf16[1,256,1280]{2,1,0:T(8,128)(2,1)} %param.22) | copy-start | bytes 1966084
  6.5 38.4 %copy-start.12 = (bf16[1,1280,320]{1,2,0:T(8,128)(2,1)S(1)}, bf16[1,1280,320]{1,2,0:T(8,128)(2,1)}, u32[]{:S(2)}) copy-start(bf16[1,1280,320]{1,2,0:T(8,128)(2,1)} %param.26) | copy-start | bytes 2457604
  6.5 40.4 %copy-start.13 = (bf16[1,1280,320]{1,2,0:T(8,128)(2,1)S(1)}, bf16[1,1280,320]{1,2,0:T(8,128)(2,1)}, u32[]{:S(2)}) copy-start(bf16[1,1280,320]{1,2,0:T(8,128)(2,1)} %param.27) | copy-start | bytes 2457604
  6.5 153.8 %all-gather.5.cloned.1.call-start = ((), (), s32[]{:S(2)}) async-start(), calls=%async_computation.8 | async-start | bytes 6604800 | tf_op jit(solution)/shard_map/all_gather | solution.py:75
  8.2 204.3 %all-gather.3.cloned.1.call-start = ((), (), s32[]{:S(2)}) async-start(), calls=%async_computation.7 | async-start | bytes 3962880 | tf_op jit(solution)/shard_map/all_gather | solution.py:119
  23.0 28.1 %all-to-all-start.1 = ((s32[128,1,2]{2,1,0:T(1,128)}), s32[128,1,2]{2,1,0:T(1,128)S(1)}, u32[]{:S(2)}, u32[]{:S(2)}) async-start(s32[128,1,2]{2,1,0:T(1,128)} %copy.47), calls=%async_computation.1 | async-start | bytes 131072 | tf_op jit(solution)/shard_map/all_to_all | solution.py:134
  40.4 21.7 %copy-start.1 = (bf16[128,1280]{1,0:T(8,128)(2,1)S(1)}, bf16[128,1280]{1,0:T(8,128)(2,1)}, u32[]{:S(2)}) copy-start(bf16[128,1280]{1,0:T(8,128)(2,1)} %param.28) | copy-start | bytes 983044
  51.1 21.6 %all-to-all-start = ((s32[128,1,1]{2,1,0:T(1,128)}), s32[128,1,1]{2,1,0:T(1,128)S(1)}, u32[]{:S(2)}, u32[]{:S(2)}) async-start(s32[128,1,1]{2,1,0:T(1,128)} %copy.45), calls=%async_computation | async-start | bytes 131072 | tf_op jit(solution)/shard_map/all_to_all | solution.py:92
  63.4 16.9 %copy-start.22 = (s32[128,1]{0,1:T(1,128)S(1)}, s32[128,1]{0,1:T(1,128)}, u32[]{:S(2)}) copy-start(s32[128,1]{0,1:T(1,128)} %param.19) | copy-start | bytes 1540
  63.4 43.5 %copy-start.18 = (bf16[320,10]{0,1:T(8,128)(2,1)S(1)}, bf16[320,10]{0,1:T(8,128)(2,1)}, u32[]{:S(2)}) copy-start(bf16[320,10]{0,1:T(8,128)(2,1)} %param.25) | copy-start | bytes 19204
  72.7 34.3 %all-to-all-start.2 = ((bf16[128,2,1280]{2,1,0:T(2,128)(2,1)}), bf16[128,2,1280]{2,1,0:T(2,128)(2,1)S(1)}, u32[]{:S(2)}, u32[]{:S(2)}) async-start(bf16[128,2,1280]{2,1,0:T(2,128)(2,1)} %reshape.356), calls=%async_computation.2 | async-start | bytes 1310720 | tf_op jit(solution)/shard_map/all_to_all | solution.py:135
  108.3 50.7 %all-to-all-start.4 = ((bf16[128,320,10]{1,2,0:T(8,128)(2,1)}), bf16[128,320,10]{1,2,0:T(8,128)(2,1)S(1)}, u32[]{:S(2)}, u32[]{:S(2)}) async-start(bf16[128,320,10]{1,2,0:T(8,128)(2,1)} %stack.2), calls=%async_computation.5 | async-start | bytes 3145728 | tf_op jit(solution)/shard_map/all_to_all | solution.py:13
  116.0 124.0 %reduce-scatter.3.cloned.1.call-start = ((), (), s32[]{:S(2)}) async-start(), calls=%async_computation.9 | async-start | bytes 819200 | tf_op jit(solution)/shard_map/reduce_scatter | solution.py:78
  123.0 37.4 %copy-start.16 = (bf16[128,1,1280]{2,0,1:T(8,128)(2,1)S(1)}, bf16[128,1,1280]{2,0,1:T(8,128)(2,1)}, u32[]{:S(2)}) copy-start(bf16[128,1,1280]{2,0,1:T(8,128)(2,1)} %param.16) | copy-start | bytes 983044
  123.0 37.4 %copy-start.26 = (f32[1280]{0:T(1024)S(1)}, f32[1280]{0:T(1024)}, u32[]{:S(2)}) copy-start(f32[1280]{0:T(1024)} %param.17) | copy-start | bytes 15364
  124.5 41.0 %copy-start.10 = (bf16[128,1280]{1,0:T(8,128)(2,1)}, bf16[128,1280]{1,0:T(8,128)(2,1)S(1)}, u32[]{:S(2)}) copy-start(bf16[128,1280]{1,0:T(8,128)(2,1)S(1)} %gather_fusion.1) | copy-start | bytes 983044
  124.5 35.9 %copy-start.29 = (f32[128]{0:T(128)S(1)}, f32[128]{0:T(128)}, u32[]{:S(2)}) copy-start(f32[128]{0:T(128)} %add_rsqrt_fusion.1) | copy-start | bytes 1540
  223.2 49.9 %copy-start.19 = (f32[1280]{0:T(1024)S(1)}, f32[1280]{0:T(1024)}, u32[]{:S(2)}) copy-start(f32[1280]{0:T(1024)} %param.23) | copy-start | bytes 15364
  223.2 49.9 %copy-start.30 = (f32[128]{0:T(128)S(1)}, f32[128]{0:T(128)}, u32[]{:S(2)}) copy-start(f32[128]{0:T(128)} %add_rsqrt_fusion.2) | copy-start | bytes 1540
  227.1 53.9 %copy-start.5 = (bf16[1,1280,320]{1,2,0:T(8,128)(2,1)}, bf16[1,1280,320]{1,2,0:T(8,128)(2,1)S(1)}, u32[]{:S(2)}) copy-start(bf16[1,1280,320]{1,2,0:T(8,128)(2,1)S(1)} %copy.64) | copy-start | bytes 2457604
  258.4 32.5 %all-to-all-start.3 = ((bf16[128,2,320]{2,1,0:T(2,128)(2,1)}), bf16[128,2,320]{2,1,0:T(2,128)(2,1)}, u32[]{:S(2)}, u32[]{:S(2)}) async-start(bf16[128,2,320]{2,1,0:T(2,128)(2,1)} %scatter_fusion.2), calls=%async_computation.4 | async-start | bytes 393216 | tf_op jit(solution)/shard_map/all_to_all | solution.py:91
  272.8 83.7 %reduce-scatter.5.cloned.1.call-start = ((), (), s32[]{:S(2)}) async-start(), calls=%async_computation.10 | async-start | bytes 1638400 | tf_op jit(solution)/shard_map/reduce_scatter | solution.py:155
  285.7 20.2 %copy-start.9 = (bf16[256,1280]{1,0:T(8,128)(2,1)S(1)}, bf16[256,1280]{1,0:T(8,128)(2,1)}, u32[]{:S(2)}) copy-start(bf16[256,1280]{1,0:T(8,128)(2,1)} %gather_fusion.2) | copy-start | bytes 1966084
  289.3 16.7 %copy-start.25 = (pred[256]{0:T(512)(128)(4,1)S(1)}, pred[256]{0:T(512)(128)(4,1)}, u32[]{:S(2)}) copy-start(pred[256]{0:T(512)(128)(4,1)} %get-tuple-element.15) | copy-start | bytes 772
  (16 other events, 112.7 us)
Sparse Core Ops, SparseCore 0:
  10.6 101.0 all-gather.4
  114.8 97.5 all-gather.2
  215.3 24.6 reduce-scatter.2
  327.3 29.2 reduce-scatter.4
